TPU v7x, 32 devices: a whole 2x2x4 slice. The times are simulated.
32 devices in a mesh: clips: 2 (over y), space: 4 (over z), tm: 2 (over x), chan: 2 (over core).
Axes of the slice: x: 2, y: 2, z: 4, core: 2. Of those that a mesh axis runs over, the one named last changes fastest.
Arguments:
- frames_in: bfloat16 [4, 16, 160, 384], P(('clips', 'tm'), 'space', None, 'chan'), parts along dimension 0, may hold values from -6 to 6
- cache: bfloat16 [4, 16, 160, 384], P('clips', 'space'), parts along dimension 0, may hold values from -6 to 6
- gain_one: bfloat16 [384], replicated, may hold values from 0.099609375 to 1.8984375
- gain_two: bfloat16 [384], replicated, may hold values from 0.099609375 to 1.8984375
- w_query: bfloat16 [384, 384], replicated, may hold values from -10 to 10
- w_key: bfloat16 [384, 384], replicated, may hold values from -10 to 10
- w_value: bfloat16 [384, 384], replicated, may hold values from -0.3125 to 0.3125
- w_out: bfloat16 [384, 384], replicated, may hold values from -0.3125 to 0.3125
- conv_weight: bfloat16 [3, 3, 3, 384, 384], P(None, None, None, None, 'chan'), may hold values from -0.0625 to 0.0625
Outputs:
- decoded: bfloat16 [4, 16, 160, 384], P(('clips', 'tm'), 'space', None, 'chan'), parts along dimension 0
There are 2 independent parts, one for each index of `clips`. A program takes and returns all parts, laid end to end along the dimension named above; an argument that names none is the same for every part. Nothing has to cross between parts.
All inputs are finite; a program needn't handle non-finite values.
Results may differ from a plain program's by a relative error of at most 0.0062.
Values may be sent and summed in bfloat16 or wider, within the bound.
A program may use at most 128 MiB of HBM per device.

v0:
```python
import jax
import jax.numpy as jnp
from jax import lax
from jax.sharding import PartitionSpec as P


def from_behind(array, axis, by):
    devices = lax.axis_size(axis)
    pairs = [(i, i + by) for i in range(devices) if 0 <= i + by < devices]
    return lax.ppermute(array, axis, pairs)


def padded_2(cells, sides, width):
    for axis, dim in sides:
        count = lax.axis_size(axis)
        ends = count - 1
        head = lax.slice_in_dim(cells, 0, width, axis=dim)
        tail = lax.slice_in_dim(cells, cells.shape[dim] - width, cells.shape[dim], axis=dim)
        cells = jnp.concatenate(
            [
                lax.ppermute(tail, axis, [(i, (i + 1) % count) for i in range(ends)]),
                cells,
                lax.ppermute(head, axis, [((i + 1) % count, i) for i in range(ends)]),
            ],
            axis=dim,
        )
    return cells


def rms_scaled(values, gain):
    wide = values.astype(jnp.float32)
    factor = lax.rsqrt(jnp.mean(wide * wide, axis=-1, keepdims=True) + 1e-06)
    return wide * factor * gain.astype(jnp.float32)


def body(frames_in, cache, gain_one, gain_two, w_query, w_key, w_value, w_out, conv_weight):
    mine = lax.axis_index("chan")
    own = lax.all_to_all(frames_in, "chan", split_axis=1, concat_axis=3, tiled=True)
    half_rows, cells, width = (own.shape[1], own.shape[2], own.shape[3])
    tokens = own.reshape(half_rows * cells, width)
    normed = rms_scaled(tokens, gain_one).astype(jnp.bfloat16)
    query = jnp.dot(normed, w_query, preferred_element_type=jnp.float32).astype(jnp.bfloat16)
    scale = width ** (-0.5)
    count = tokens.shape[0]
    piece = lax.all_gather(normed, ("space", "chan"), axis=0, tiled=True)
    keys = jnp.dot(piece, w_key, preferred_element_type=jnp.float32).astype(jnp.bfloat16)
    values = jnp.dot(piece, w_value, preferred_element_type=jnp.float32).astype(jnp.bfloat16)
    top = jnp.full((count, 1), -1e30, jnp.float32)
    scores = jnp.einsum("qc,kc->qk", query, keys, preferred_element_type=jnp.float32) * scale
    new_top = jnp.maximum(top, jnp.max(scores, axis=-1, keepdims=True))
    weights = jnp.exp(scores - new_top)
    total = jnp.sum(weights, axis=-1, keepdims=True)
    accum = jnp.dot(weights.astype(jnp.bfloat16), values, preferred_element_type=jnp.float32)
    top, total, accum = (new_top, total, accum)
    attended = (accum / total).astype(jnp.bfloat16)
    joined = tokens.astype(jnp.float32) + jnp.dot(
        attended, w_out, preferred_element_type=jnp.float32
    )
    joined = joined.astype(jnp.bfloat16).reshape(1, half_rows, cells, width)
    whole = lax.all_gather(joined, "chan", axis=1, tiled=True)
    act = jax.nn.silu(rms_scaled(whole, gain_two)).astype(jnp.bfloat16)
    moment = lax.axis_index("tm")
    first = from_behind(act, "tm", 1)
    second = from_behind(act, "tm", 2)
    prev_one = jnp.where(moment == 0, cache[1:2], first)
    prev_two = jnp.where(moment == 0, cache[0:1], jnp.where(moment == 1, cache[1:2], second))
    stacked = jnp.concatenate([prev_two, prev_one, act], axis=0)
    rimmed = padded_2(stacked, (("space", 1),), 1)
    padded = jnp.pad(rimmed, ((0, 0), (0, 0), (1, 1), (0, 0)))
    conv = lax.conv_general_dilated(
        padded[None],
        conv_weight,
        (1, 1, 1),
        "VALID",
        dimension_numbers=("NDHWC", "DHWIO", "NDHWC"),
        preferred_element_type=jnp.float32,
    )[0]
    share = conv_weight.shape[4]
    own_joined = lax.dynamic_slice_in_dim(whole, mine * share, share, 3)
    return (own_joined.astype(jnp.float32) + conv).astype(jnp.bfloat16)


def solution(mesh):
    return jax.shard_map(
        body,
        mesh=mesh,
        in_specs=(
            P(("clips", "tm"), "space", None, "chan"),
            P("clips", "space", None, None),
            P(),
            P(),
            P(),
            P(),
            P(),
            P(),
            P(None, None, None, None, "chan"),
        ),
        out_specs=P(("clips", "tm"), "space", None, "chan"),
        check_vma=False,
    )
```

profile of v0, /device:TPU:0, one launch (start us, length us, event | category | flops | bytes accessed | tf_op | source)
XLA Modules:
  0.0 116.3 jit_solution(1926624197613109839)
XLA Ops:
  6.6 5.2 %all_to_all.4 = bf16[1,4,160,192]{3,2,0,1:T(8,128)(2,1)S(1)} all-to-all(bf16[1,4,160,192]{3,2,0,1:T(8,128)(2,1)} %bitcast.55), channel_id=1, replica_groups=mesh['clips'=2,'space'=4,'tm'=2,'chan'=2] {'chan'}, dimensions={1} | all-to-all | bytes 491520 | tf_op jit(solution)/shard_map/all_to_all | solution.py:38
  12.1 0.5 reshape.60
  13.0 0.8 multiply_convert_fusion
  13.8 1.3 %convolution_convert_fusion.2 = bf16[320,384]{1,0:T(8,128)(2,1)S(1)} fusion(bf16[320,384]{1,0:T(8,128)(2,1)} %multiply_convert_fusion, bf16[384,384]{1,0:T(8,128)(2,1)S(1)} %copy-done.2), kind=kOutput, calls=%fused_computation.32 | convolution fusion | flops 94494720 | bytes 786432 | tf_op jit(solution)/shard_map/dot_general | solution.py:42
  15.1 29.6 %all-gather.2.cloned.1.call-done = bf16[2560,384]{1,0:T(8,128)(2,1)} async-done(((bf16[320,384]{1,0:T(8,128)(2,1)}), bf16[2560,384]{1,0:T(8,128)(2,1)}) %all-gather.2.cloned.1.call-update) | async-done | bytes 1966096 | tf_op jit(solution)/shard_map/all_gather | solution.py:45
  44.7 5.4 %fusion.46 = (f32[320]{0:T(512)S(1)}, f32[320,2560]{1,0:T(8,128)}) fusion(bf16[320,384]{1,0:T(8,128)(2,1)S(1)} %convolution_convert_fusion.2, bf16[2560,384]{1,0:T(8,128)(2,1)} %all-gather.2.cloned.1.call-done, bf16[384,384]{1,0:T(8,128)(2,1)S(1)} %copy-done), kind=kOutput, calls=%fused_computation.64 | convolution fusion | flops 1386741504 | bytes 5784832 | tf_op jit(solution)/shard_map/qc,kc->qk/dot_general | solution.py:49
  50.1 2.6 %fusion.2 = f32[320]{0:T(512)S(1)} fusion(f32[320,2560]{1,0:T(8,128)} %get-tuple-element.10, f32[320]{0:T(512)S(1)} %broadcast_maximum_fusion), kind=kLoop, calls=%fused_computation.9 | loop fusion | flops 1638080 | bytes 3279360 | tf_op jit(solution)/shard_map/reduce_sum | solution.py:52
  52.7 4.8 %fusion.28 = bf16[320,384]{1,0:T(8,128)(2,1)S(1)} fusion(f32[320,2560]{1,0:T(8,128)} %get-tuple-element.10, f32[320]{0:T(512)S(1)} %broadcast_maximum_fusion, bf16[2560,384]{1,0:T(8,128)(2,1)} %all-gather.2.cloned.1.call-done, bf16[384,384]{1,0:T(8,128)(2,1)S(1)} %copy-done.7, f32[320]{0:T(512)S(1)} %fusion.2), kind=kOutput, calls=%fused_computation.35 | convolution fusion | flops 1386987520 | bytes 5786112 | tf_op jit(solution)/shard_map/dot_general | solution.py:53
  57.9 2.2 %all_gather.7 = bf16[1,4,160,384]{3,2,0,1:T(8,128)(2,1)S(1)} all-gather(bf16[1,2,160,384]{3,2,0,1:T(8,128)(2,1)S(1)} %bitcast.53), channel_id=1, replica_groups=mesh['clips'=2,'space'=4,'tm'=2,'chan'=2] {'chan'}, dimensions={1}, use_global_device_ids=true | all-gather | bytes 737280 | tf_op jit(solution)/shard_map/all_gather | solution.py:60
  60.6 1.4 %collective-permute-start = (bf16[1,4,160,384]{3,2,0,1:T(8,128)(2,1)S(1)}, bf16[1,4,160,384]{3,2,0,1:T(8,128)(2,1)}, u32[]{:S(2)}, u32[]{:S(2)}) collective-permute-start(bf16[1,4,160,384]{3,2,0,1:T(8,128)(2,1)S(1)} %fusion.38), channel_id=1, source_target_pairs={} | collective-permute-start | bytes 1474568 | tf_op jit(solution)/shard_map/ppermute | solution.py:10
  62.1 4.2 %collective-permute-start.1 = (bf16[1,4,160,384]{3,2,0,1:T(8,128)(2,1)S(1)}, bf16[1,4,160,384]{3,2,0,1:T(8,128)(2,1)}, u32[]{:S(2)}, u32[]{:S(2)}) collective-permute-start(bf16[1,4,160,384]{3,2,0,1:T(8,128)(2,1)S(1)} %fusion.38), channel_id=1, source_target_pairs={{0,2},{1,3},{4,6},{5,7},{8,10},{9,11},{12,14},{13,15},{16,18},{17,... | collective-permute-start | bytes 1474568 | tf_op jit(solution)/shard_map/ppermute | solution.py:10
  66.2 10.1 %collective-permute-done.1 = bf16[1,4,160,384]{3,2,0,1:T(8,128)(2,1)} collective-permute-done((bf16[1,4,160,384]{3,2,0,1:T(8,128)(2,1)S(1)}, bf16[1,4,160,384]{3,2,0,1:T(8,128)(2,1)}, u32[]{:S(2)}, u32[]{:S(2)}) %collective-permute-start.1) | collective-permute-done | bytes 491552 | tf_op jit(solution)/shard_map/ppermute | solution.py:10
  76.3 1.1 fusion.41
  77.5 1.0 maximum_bitcast_fusion
  78.4 3.5 %collective-permute-start.2 = (bf16[3,1,160,384]{3,2,1,0:T(8,128)(2,1)}, bf16[3,1,160,384]{3,2,1,0:T(8,128)(2,1)S(1)}, u32[]{:S(2)}, u32[]{:S(2)}) collective-permute-start(bf16[3,1,160,384]{3,2,1,0:T(8,128)(2,1)} %get-tuple-element.5), channel_id=1, source_target_pairs={{0,4},{4,8},{8,12},{1,5},{5,9},{9,13},{2,6},{6,10},{10,14},{3,7},{... | collective-permute-start | bytes 1105928 | tf_op jit(solution)/shard_map/ppermute | solution.py:21
  81.9 1.5 %collective-permute-start.3 = (bf16[3,1,160,384]{3,2,1,0:T(8,128)(2,1)}, bf16[3,1,160,384]{3,2,1,0:T(8,128)(2,1)}, u32[]{:S(2)}, u32[]{:S(2)}) collective-permute-start(bf16[3,1,160,384]{3,2,1,0:T(8,128)(2,1)} %get-tuple-element.6), channel_id=1, source_target_pairs={{4,0},{8,4},{12,8},{5,1},{9,5},{13,9},{6,2},{10,6},{14,10},{7,3},{... | collective-permute-start | bytes 1105928 | tf_op jit(solution)/shard_map/ppermute | solution.py:23
  83.6 6.1 %collective-permute-done.2 = bf16[3,1,160,384]{3,2,1,0:T(8,128)(2,1)S(1)} collective-permute-done((bf16[3,1,160,384]{3,2,1,0:T(8,128)(2,1)}, bf16[3,1,160,384]{3,2,1,0:T(8,128)(2,1)S(1)}, u32[]{:S(2)}, u32[]{:S(2)}) %collective-permute-start.2) | collective-permute-done | bytes 368672 | tf_op jit(solution)/shard_map/ppermute | solution.py:21
  89.7 4.1 %collective-permute-done.3 = bf16[3,1,160,384]{3,2,1,0:T(8,128)(2,1)} collective-permute-done((bf16[3,1,160,384]{3,2,1,0:T(8,128)(2,1)}, bf16[3,1,160,384]{3,2,1,0:T(8,128)(2,1)}, u32[]{:S(2)}, u32[]{:S(2)}) %collective-permute-start.3) | collective-permute-done | bytes 368672 | tf_op jit(solution)/shard_map/ppermute | solution.py:23
  93.8 3.1 %fusion.11 = bf16[3,6,1,162,384]{4,3,0,1,2:T(8,128)(2,1)S(1)} fusion(bf16[3,1,160,384]{3,2,0,1:T(8,128)(2,1)} %bitcast.8, bf16[3,1,160,384]{3,2,0,1:T(8,128)(2,1)S(1)} %bitcast.54, bf16[1,4,160,384]{3,2,0,1:T(8,128)(2,1)S(1)} %fusion.38, bf16[1,4,160,384]{3,2,0,1:T(8,128)(2,1)S(1)} %get-tuple-element.8, bf16[1,4,160,384]{3,2,0,1:T(8,128)(2,1)S(1)} %get-tuple-element.7), kind=kLoop, calls=%fused_computation.18 | loop fusion | flops 20155392 | bytes 4451328 | tf_op jit(solution)/shard_map/broadcast_in_dim | solution.py:71
  96.9 1.6 %pad.5 = bf16[3,6,1,168,384]{4,3,0,1,2:T(8,128)(2,1)} pad(bf16[3,6,1,162,384]{4,3,0,1,2:T(8,128)(2,1)S(1)} %fusion.11, bf16[]{:T(256)} %constant.34.clone.1), padding=0_0x0_0x0_0x0_6x0_0 | pad | bytes 4561922 | tf_op jit(solution)/shard_map/broadcast_in_dim | solution.py:71
  98.5 3.5 %reshape.69 = bf16[3,6,1,8,21,384]{5,4,3,0,1,2:T(8,128)(2,1)S(1)} reshape(bf16[3,6,1,168,384]{4,3,0,1,2:T(8,128)(2,1)} %pad.5) | data formatting | bytes 4644864 | tf_op jit(solution)/shard_map/conv_general_dilated | solution.py:70
  102.4 1.7 %copy-done.6 = bf16[3,3,3,384,192]{3,4,2,1,0:T(8,128)(2,1)S(1)} copy-done((bf16[3,3,3,384,192]{3,4,2,1,0:T(8,128)(2,1)S(1)}, bf16[3,3,3,384,192]{3,4,2,1,0:T(8,128)(2,1)}, u32[]{:S(2)}) %copy-start.6) | copy-done | bytes 3981336
  104.2 3.9 %fusion.21 = f32[1,4,8,21,192]{4,2,3,1,0:T(8,128)S(1)} fusion(bf16[3,3,3,384,192]{3,4,2,1,0:T(8,128)(2,1)S(1)} %copy-done.6, bf16[3,6,1,7,2,384]{5,3,4,1,0,2:T(8,128)(2,1)S(1)} %slice.19, bf16[3,6,1,8,21,384]{5,3,4,1,0,2:T(8,128)(2,1)S(1)} %copy.47, pred[8,21]{0,1:T(8,128)(4,1)S(1)} %copy-done.8), kind=kOutput, calls=%fused_computation.28 | convolution fusion | flops 2683201536 | bytes 7013544 | tf_op jit(solution)/shard_map/conv_general_dilated | solution.py:70
  108.7 0.8 copy.49
  (38 shorter events, 2.8 us)
Async XLA Ops:
  6.5 38.2 %copy-start = (bf16[384,384]{1,0:T(8,128)(2,1)S(1)}, bf16[384,384]{1,0:T(8,128)(2,1)}, u32[]{:S(2)}) copy-start(bf16[384,384]{1,0:T(8,128)(2,1)} %param.14) | copy-start | bytes 884740
  6.5 6.4 %copy-start.4 = (bf16[384]{0:T(512)(128)(2,1)S(1)}, bf16[384]{0:T(512)(128)(2,1)}, u32[]{:S(2)}) copy-start(bf16[384]{0:T(512)(128)(2,1)} %param.11) | copy-start | bytes 2308
  6.5 7.3 %copy-start.5 = (bf16[384]{0:T(512)(128)(2,1)S(1)}, bf16[384]{0:T(512)(128)(2,1)}, u32[]{:S(2)}) copy-start(bf16[384]{0:T(512)(128)(2,1)} %param.12) | copy-start | bytes 2308
  6.5 7.3 %copy-start.2 = (bf16[384,384]{1,0:T(8,128)(2,1)S(1)}, bf16[384,384]{1,0:T(8,128)(2,1)}, u32[]{:S(2)}) copy-start(bf16[384,384]{1,0:T(8,128)(2,1)} %param.13) | copy-start | bytes 884740
  6.5 38.1 %all-gather.2.cloned.1.call-start = ((), (), s32[]{:S(2)}) async-start(), calls=%async_computation.1 | async-start | bytes 2211840 | tf_op jit(solution)/shard_map/all_gather | solution.py:45
  50.1 2.6 %copy-start.7 = (bf16[384,384]{1,0:T(8,128)(2,1)S(1)}, bf16[384,384]{1,0:T(8,128)(2,1)}, u32[]{:S(2)}) copy-start(bf16[384,384]{1,0:T(8,128)(2,1)} %param.15) | copy-start | bytes 884740
  52.7 4.8 %copy-start.3 = (bf16[384,384]{1,0:T(8,128)(2,1)S(1)}, bf16[384,384]{1,0:T(8,128)(2,1)}, u32[]{:S(2)}) copy-start(bf16[384,384]{1,0:T(8,128)(2,1)} %param.16) | copy-start | bytes 884740
  57.5 18.8 %copy-start.1 = (bf16[2,4,160,384]{3,2,1,0:T(8,128)(2,1)S(1)}, bf16[2,4,160,384]{3,2,1,0:T(8,128)(2,1)}, u32[]{:S(2)}) copy-start(bf16[2,4,160,384]{3,2,1,0:T(8,128)(2,1)} %param.10) | copy-start | bytes 2949124
  60.6 5.6 %collective-permute-start = (bf16[1,4,160,384]{3,2,0,1:T(8,128)(2,1)S(1)}, bf16[1,4,160,384]{3,2,0,1:T(8,128)(2,1)}, u32[]{:S(2)}, u32[]{:S(2)}) collective-permute-start(bf16[1,4,160,384]{3,2,0,1:T(8,128)(2,1)S(1)} %fusion.38), channel_id=1, source_target_pairs={} | collective-permute-start | bytes 1474568 | tf_op jit(solution)/shard_map/ppermute | solution.py:10
  62.1 14.2 %collective-permute-start.1 = (bf16[1,4,160,384]{3,2,0,1:T(8,128)(2,1)S(1)}, bf16[1,4,160,384]{3,2,0,1:T(8,128)(2,1)}, u32[]{:S(2)}, u32[]{:S(2)}) collective-permute-start(bf16[1,4,160,384]{3,2,0,1:T(8,128)(2,1)S(1)} %fusion.38), channel_id=1, source_target_pairs={{0,2},{1,3},{4,6},{5,7},{8,10},{9,11},{12,14},{13,15},{16,18},{17,... | collective-permute-start | bytes 1474568 | tf_op jit(solution)/shard_map/ppermute | solution.py:10
  78.4 11.2 %collective-permute-start.2 = (bf16[3,1,160,384]{3,2,1,0:T(8,128)(2,1)}, bf16[3,1,160,384]{3,2,1,0:T(8,128)(2,1)S(1)}, u32[]{:S(2)}, u32[]{:S(2)}) collective-permute-start(bf16[3,1,160,384]{3,2,1,0:T(8,128)(2,1)} %get-tuple-element.5), channel_id=1, source_target_pairs={{0,4},{4,8},{8,12},{1,5},{5,9},{9,13},{2,6},{6,10},{10,14},{3,7},{... | collective-permute-start | bytes 1105928 | tf_op jit(solution)/shard_map/ppermute | solution.py:21
  81.9 11.9 %collective-permute-start.3 = (bf16[3,1,160,384]{3,2,1,0:T(8,128)(2,1)}, bf16[3,1,160,384]{3,2,1,0:T(8,128)(2,1)}, u32[]{:S(2)}, u32[]{:S(2)}) collective-permute-start(bf16[3,1,160,384]{3,2,1,0:T(8,128)(2,1)} %get-tuple-element.6), channel_id=1, source_target_pairs={{4,0},{8,4},{12,8},{5,1},{9,5},{13,9},{6,2},{10,6},{14,10},{7,3},{... | collective-permute-start | bytes 1105928 | tf_op jit(solution)/shard_map/ppermute | solution.py:23
  102.0 2.1 %copy-start.6 = (bf16[3,3,3,384,192]{3,4,2,1,0:T(8,128)(2,1)S(1)}, bf16[3,3,3,384,192]{3,4,2,1,0:T(8,128)(2,1)}, u32[]{:S(2)}) copy-start(bf16[3,3,3,384,192]{3,4,2,1,0:T(8,128)(2,1)} %param.17) | copy-start | bytes 11943940
  102.0 2.1 %copy-start.8 = (pred[8,21]{0,1:T(8,128)(4,1)S(1)}, pred[8,21]{0,1:T(8,128)(4,1)}, u32[]{:S(2)}) copy-start(pred[8,21]{0,1:T(8,128)(4,1)} %constant.42) | copy-start | bytes 508
Sparse Core Ops, SparseCore 0:
  13.9 30.7 all-gather.1
where the time goes:
time: 117 us; the launch traced here: 116 us
  waiting for transfers between devices  49.9 us (43%)
  matrix products  15.7 us (13%)
  between operations  13.6 us (12%)
  starting transfers between devices  10.6 us (9%)
  other arithmetic  9.76 us (8%)
  local copies, waits for them, and re-layouts  9.41 us (8%)
  blocking collectives  7.34 us (6%)
    all_gather x1, waiting for transfers between devices, body(): piece = lax.all_gather(normed, ('space', 'chan'), axis=0, tiled=True)  29.6 us
    ppermute x2, waiting for transfers between devices, from_behind(): return lax.ppermute(array, axis, pairs)  10.1 us
    ppermute x1, waiting for transfers between devices, padded_2(): lax.ppermute(tail, axis, [(i, (i + 1) % count) for i in range(ends)])  6.08 us
    ppermute x2, starting transfers between devices, from_behind(): return lax.ppermute(array, axis, pairs)  5.6 us
    dot_general x1, matrix products, body(): jnp.einsum('qc,kc->qk', query, keys, preferred_element_type=jnp.float32)  5.41 us
    all_to_all x1, blocking collectives, body(): lax.all_to_all(frames_in, 'chan', split_axis=1, concat_axis=3, tiled=True)  5.19 us
    dot_general x1, matrix products, body(): jnp.dot(weights.astype(jnp.bfloat16), values, preferred_element_type=jnp....  4.79 us
    ppermute x1, waiting for transfers between devices, padded_2(): lax.ppermute(head, axis, [((i + 1) % count, i) for i in range(ends)])  4.14 us
  transfers between devices with their start and end apart: 5, of which 4 were waited for; matrix products, arithmetic and copies ran while one was open for 1% of the time, Pallas kernels for 0%

commit v1 on v0

--- a/solution.py
+++ b/solution.py
@@ -2,6 +2,35 @@
 import jax.numpy as jnp
 from jax import lax
 from jax.sharding import PartitionSpec as P
+
+
+def link_map(w_in, array_axis):
+    w_in = jnp.moveaxis(w_in, 0, array_axis)
+    aux = w_in.shape
+    earlier = w_in.reshape(
+        *aux[:array_axis], aux[array_axis] * aux[array_axis + 1], *aux[array_axis + 2 :]
+    )
+    return earlier
+
+
+def view_raise(in_array, mesh_name):
+    built = lax.axis_size(mesh_name)
+    r2, tmp = (built, lax.axis_index(mesh_name))
+    oldest, t1 = (in_array[None], 1)
+    while t1 < r2:
+        panels = []
+        for h in range(r2):
+            panels.append((h, h ^ t1))
+        y2 = lax.ppermute(oldest, mesh_name, panels)
+        y1 = tmp & t1 == 0
+        oldest = jnp.concatenate([jnp.where(y1, oldest, y2), jnp.where(y1, y2, oldest)])
+        t1 *= 2
+    return oldest
+
+
+def column_do(arr, x_local, dim_at):
+    part_now = link_map(view_raise(arr, x_local), dim_at)
+    return part_now
 
 
 def from_behind(array, axis, by):
@@ -42,7 +71,7 @@
     query = jnp.dot(normed, w_query, preferred_element_type=jnp.float32).astype(jnp.bfloat16)
     scale = width ** (-0.5)
     count = tokens.shape[0]
-    piece = lax.all_gather(normed, ("space", "chan"), axis=0, tiled=True)
+    piece = column_do(normed, ("space", "chan"), 0)
     keys = jnp.dot(piece, w_key, preferred_element_type=jnp.float32).astype(jnp.bfloat16)
     values = jnp.dot(piece, w_value, preferred_element_type=jnp.float32).astype(jnp.bfloat16)
     top = jnp.full((count, 1), -1e30, jnp.float32)

time: 117 us -> 133 us (1.14)
  waiting for transfers between devices: 49.9 us -> 73.7 us
  between operations: 13.6 us -> 0.27 us
  starting transfers between devices: 10.6 us -> 15.5 us
  matrix products: 15.7 us -> 13.7 us
  other arithmetic: 9.76 us -> 11.2 us
    ppermute x0 -> x3, waiting for transfers between devices: none -> 53.6 us  [view_raise(): y2 = lax.ppermute(oldest, mesh_name, panels)]
    all_gather x1 -> x0, waiting for transfers between devices: 29.6 us -> none  [body(): piece = lax.all_gather(normed, ('space', 'chan'), axis=0, tiled=True)]
    ppermute x0 -> x3, starting transfers between devices: none -> 6.12 us  [view_raise(): y2 = lax.ppermute(oldest, mesh_name, panels)]
    select_n x0 -> x3, other arithmetic: none -> 1.76 us  [view_raise(): jnp.where(y1, oldest, y2)]
    dot_general x1, matrix products: 5.41 us -> 3.89 us  [body(): jnp.einsum('qc,kc->qk', query, keys, preferred_element_type=jnp.float32)]
  transfers between devices with their start and end apart: 5 -> 7, of which waited for: 4 -> 6; matrix products, arithmetic and copies ran while one was open for 1% -> 2% of each run, Pallas kernels for 0% -> 0%
where the time goes in v1:
time: 133 us; the launch traced here: 132 us
  waiting for transfers between devices  73.7 us (55%)
  starting transfers between devices  15.5 us (12%)
  matrix products  13.7 us (10%)
  other arithmetic  11.2 us (8%)
  local copies, waits for them, and re-layouts  9.9 us (7%)
  blocking collectives  7.33 us (6%)
    ppermute x3, waiting for transfers between devices, view_raise(): y2 = lax.ppermute(oldest, mesh_name, panels)  53.6 us
    ppermute x2, waiting for transfers between devices, from_behind(): return lax.ppermute(array, axis, pairs)  9.99 us
    ppermute x3, starting transfers between devices, view_raise(): y2 = lax.ppermute(oldest, mesh_name, panels)  6.12 us
    ppermute x1, waiting for transfers between devices, padded_2(): lax.ppermute(tail, axis, [(i, (i + 1) % count) for i in range(ends)])  5.94 us
    ppermute x2, starting transfers between devices, from_behind(): return lax.ppermute(array, axis, pairs)  5.45 us
    all_to_all x1, blocking collectives, body(): lax.all_to_all(frames_in, 'chan', split_axis=1, concat_axis=3, tiled=True)  5.17 us
    dot_general x1, matrix products, body(): jnp.dot(weights.astype(jnp.bfloat16), values, preferred_element_type=jnp....  4.21 us
    ppermute x1, waiting for transfers between devices, padded_2(): lax.ppermute(head, axis, [((i + 1) % count, i) for i in range(ends)])  4.14 us
  transfers between devices with their start and end apart: 7, of which 6 were waited for; matrix products, arithmetic and copies ran while one was open for 2% of the time, Pallas kernels for 0%

profile of v1, /device:TPU:0, one launch (start us, length us, event | category | flops | bytes accessed | tf_op | source)
XLA Modules:
  0.0 131.6 jit_solution(1793169788023028562)
XLA Ops:
  0.0 5.2 %all_to_all.4 = bf16[1,4,160,192]{3,2,0,1:T(8,128)(2,1)S(1)} all-to-all(bf16[1,4,160,192]{3,2,0,1:T(8,128)(2,1)} %bitcast.58), channel_id=1, replica_groups=mesh['clips'=2,'space'=4,'tm'=2,'chan'=2] {'chan'}, dimensions={1} | all-to-all | bytes 491520 | tf_op jit(solution)/shard_map/all_to_all | solution.py:67
  6.7 1.4 %collective-permute-done = bf16[1,320,384]{2,1,0:T(8,128)(2,1)S(1)} collective-permute-done((bf16[1,320,384]{2,1,0:T(8,128)(2,1)S(1)}, bf16[1,320,384]{2,1,0:T(8,128)(2,1)S(1)}, u32[]{:S(2)}, u32[]{:S(2)}) %collective-permute-start) | collective-permute-done | bytes 245792 | tf_op jit(solution)/shard_map/ppermute | solution.py:24
  8.3 3.1 %collective-permute-start.1 = (bf16[2,320,384]{2,1,0:T(8,128)(2,1)S(1)}, bf16[2,320,384]{2,1,0:T(8,128)(2,1)S(1)}, u32[]{:S(2)}, u32[]{:S(2)}) collective-permute-start(bf16[2,320,384]{2,1,0:T(8,128)(2,1)S(1)} %pad_maximum_fusion.2), channel_id=1, source_target_pairs={{0,4},{1,5},{4,0},{5,1},{8,12},{9,13},{12,8},{13,9},{2,6},{3,7},{6... | collective-permute-start | bytes 1474568 | tf_op jit(solution)/shard_map/ppermute | solution.py:24
  11.4 11.5 %collective-permute-done.1 = bf16[2,320,384]{2,1,0:T(8,128)(2,1)S(1)} collective-permute-done((bf16[2,320,384]{2,1,0:T(8,128)(2,1)S(1)}, bf16[2,320,384]{2,1,0:T(8,128)(2,1)S(1)}, u32[]{:S(2)}, u32[]{:S(2)}) %collective-permute-start.1) | collective-permute-done | bytes 491552 | tf_op jit(solution)/shard_map/ppermute | solution.py:24
  23.2 2.8 %collective-permute-start.2 = (bf16[4,320,384]{2,1,0:T(8,128)(2,1)S(1)}, bf16[4,320,384]{2,1,0:T(8,128)(2,1)}, u32[]{:S(2)}, u32[]{:S(2)}) collective-permute-start(bf16[4,320,384]{2,1,0:T(8,128)(2,1)S(1)} %pad_maximum_fusion.1), channel_id=1, source_target_pairs={{0,8},{1,9},{4,12},{5,13},{8,0},{9,1},{12,4},{13,5},{2,10},{3,11},... | collective-permute-start | bytes 2949128 | tf_op jit(solution)/shard_map/ppermute | solution.py:24
  26.6 1.3 %convolution_convert_fusion.2 = bf16[320,384]{1,0:T(8,128)(2,1)S(1)} fusion(bf16[384,384]{1,0:T(8,128)(2,1)} %param.13, f32[320,384]{1,0:T(8,128)S(1)} %reshape.126, f32[384]{0:T(512)S(1)} %convert_element_type.87, f32[320]{0:T(512)S(1)} %rsqrt.20), kind=kOutput, calls=%fused_computation.33 | convolution fusion | flops 94863360 | bytes 1035008 | tf_op jit(solution)/shard_map/dot_general | solution.py:71
  27.9 40.7 %collective-permute-done.2 = bf16[4,320,384]{2,1,0:T(8,128)(2,1)} collective-permute-done((bf16[4,320,384]{2,1,0:T(8,128)(2,1)S(1)}, bf16[4,320,384]{2,1,0:T(8,128)(2,1)}, u32[]{:S(2)}, u32[]{:S(2)}) %collective-permute-start.2) | collective-permute-done | bytes 983072 | tf_op jit(solution)/shard_map/ppermute | solution.py:24
  68.6 1.5 %broadcast_select_fusion.1 = (bf16[4,320,384]{2,1,0:T(8,128)(2,1)S(1)}, bf16[4,320,384]{2,1,0:T(8,128)(2,1)S(1)}) fusion(bf16[4,320,384]{2,1,0:T(8,128)(2,1)} %collective-permute-done.2, pred[]{:T(512)S(6)} %eq.16, bf16[2,320,384]{2,1,0:T(8,128)(2,1)S(1)} %get-tuple-element.12, bf16[2,320,384]{2,1,0:T(8,128)(2,1)S(1)} %get-tuple-element.11), kind=kLoop, calls=%fused_computation.47 | loop fusion | flops 1474560 | bytes 3932161 | tf_op jit(solution)/shard_map/jit(_where)/select_n | solution.py:26
  70.3 3.9 %fusion.48 = (f32[320]{0:T(512)S(1)}, f32[320,2560]{1,0:T(8,128)}) fusion(bf16[320,384]{1,0:T(8,128)(2,1)S(1)} %convolution_convert_fusion.2, bf16[2560,384]{1,0:T(8,128)(2,1)S(1)} %bitcast.54, bf16[384,384]{1,0:T(8,128)(2,1)S(1)} %copy-done), kind=kOutput, calls=%fused_computation.76 | convolution fusion | flops 1386741504 | bytes 5784832 | tf_op jit(solution)/shard_map/qc,kc->qk/dot_general | solution.py:78
  74.2 2.5 %fusion.2 = f32[320]{0:T(512)S(1)} fusion(f32[320,2560]{1,0:T(8,128)} %get-tuple-element.16, f32[320]{0:T(512)S(1)} %broadcast_maximum_fusion), kind=kLoop, calls=%fused_computation.9 | loop fusion | flops 1638080 | bytes 3279360 | tf_op jit(solution)/shard_map/reduce_sum | solution.py:81
  76.8 4.2 %fusion.28 = bf16[320,384]{1,0:T(8,128)(2,1)S(1)} fusion(f32[320,2560]{1,0:T(8,128)} %get-tuple-element.16, f32[320]{0:T(512)S(1)} %broadcast_maximum_fusion, bf16[2560,384]{1,0:T(8,128)(2,1)S(1)} %bitcast.55, bf16[384,384]{1,0:T(8,128)(2,1)} %param.15, f32[320]{0:T(512)S(1)} %fusion.2), kind=kOutput, calls=%fused_computation.36 | convolution fusion | flops 1386987520 | bytes 5786112 | tf_op jit(solution)/shard_map/dot_general | solution.py:82
  81.3 2.2 %all_gather.3 = bf16[1,4,160,384]{3,2,0,1:T(8,128)(2,1)S(1)} all-gather(bf16[1,2,160,384]{3,2,0,1:T(8,128)(2,1)S(1)} %bitcast.56), channel_id=1, replica_groups=mesh['clips'=2,'space'=4,'tm'=2,'chan'=2] {'chan'}, dimensions={1}, use_global_device_ids=true | all-gather | bytes 737280 | tf_op jit(solution)/shard_map/all_gather | solution.py:89
  84.1 1.4 %collective-permute-start.3 = (bf16[1,4,160,384]{3,2,0,1:T(8,128)(2,1)S(1)}, bf16[1,4,160,384]{3,2,0,1:T(8,128)(2,1)}, u32[]{:S(2)}, u32[]{:S(2)}) collective-permute-start(bf16[1,4,160,384]{3,2,0,1:T(8,128)(2,1)S(1)} %fusion.38), channel_id=1, source_target_pairs={} | collective-permute-start | bytes 1474568 | tf_op jit(solution)/shard_map/ppermute | solution.py:39
  85.6 4.0 %collective-permute-start.4 = (bf16[1,4,160,384]{3,2,0,1:T(8,128)(2,1)S(1)}, bf16[1,4,160,384]{3,2,0,1:T(8,128)(2,1)}, u32[]{:S(2)}, u32[]{:S(2)}) collective-permute-start(bf16[1,4,160,384]{3,2,0,1:T(8,128)(2,1)S(1)} %fusion.38), channel_id=1, source_target_pairs={{0,2},{1,3},{4,6},{5,7},{8,10},{9,11},{12,14},{13,15},{16,18},{17,... | collective-permute-start | bytes 1474568 | tf_op jit(solution)/shard_map/ppermute | solution.py:39
  89.6 10.0 %collective-permute-done.4 = bf16[1,4,160,384]{3,2,0,1:T(8,128)(2,1)} collective-permute-done((bf16[1,4,160,384]{3,2,0,1:T(8,128)(2,1)S(1)}, bf16[1,4,160,384]{3,2,0,1:T(8,128)(2,1)}, u32[]{:S(2)}, u32[]{:S(2)}) %collective-permute-start.4) | collective-permute-done | bytes 491552 | tf_op jit(solution)/shard_map/ppermute | solution.py:39
  101.7 2.5 %collective-permute-start.5 = (bf16[3,1,160,384]{3,2,1,0:T(8,128)(2,1)}, bf16[3,1,160,384]{3,2,1,0:T(8,128)(2,1)S(1)}, u32[]{:S(2)}, u32[]{:S(2)}) collective-permute-start(bf16[3,1,160,384]{3,2,1,0:T(8,128)(2,1)} %get-tuple-element.7), channel_id=1, source_target_pairs={{0,4},{4,8},{8,12},{1,5},{5,9},{9,13},{2,6},{6,10},{10,14},{3,7},{... | collective-permute-start | bytes 1105928 | tf_op jit(solution)/shard_map/ppermute | solution.py:50
  104.2 1.5 %collective-permute-start.6 = (bf16[3,1,160,384]{3,2,1,0:T(8,128)(2,1)}, bf16[3,1,160,384]{3,2,1,0:T(8,128)(2,1)}, u32[]{:S(2)}, u32[]{:S(2)}) collective-permute-start(bf16[3,1,160,384]{3,2,1,0:T(8,128)(2,1)} %get-tuple-element.8), channel_id=1, source_target_pairs={{4,0},{8,4},{12,8},{5,1},{9,5},{13,9},{6,2},{10,6},{14,10},{7,3},{... | collective-permute-start | bytes 1105928 | tf_op jit(solution)/shard_map/ppermute | solution.py:52
  105.8 5.9 %collective-permute-done.5 = bf16[3,1,160,384]{3,2,1,0:T(8,128)(2,1)S(1)} collective-permute-done((bf16[3,1,160,384]{3,2,1,0:T(8,128)(2,1)}, bf16[3,1,160,384]{3,2,1,0:T(8,128)(2,1)S(1)}, u32[]{:S(2)}, u32[]{:S(2)}) %collective-permute-start.5) | collective-permute-done | bytes 368672 | tf_op jit(solution)/shard_map/ppermute | solution.py:50
  111.8 4.1 %collective-permute-done.6 = bf16[3,1,160,384]{3,2,1,0:T(8,128)(2,1)} collective-permute-done((bf16[3,1,160,384]{3,2,1,0:T(8,128)(2,1)}, bf16[3,1,160,384]{3,2,1,0:T(8,128)(2,1)}, u32[]{:S(2)}, u32[]{:S(2)}) %collective-permute-start.6) | collective-permute-done | bytes 368672 | tf_op jit(solution)/shard_map/ppermute | solution.py:52
  115.9 3.1 %fusion.11 = bf16[3,6,1,162,384]{4,3,0,1,2:T(8,128)(2,1)S(1)} fusion(bf16[3,1,160,384]{3,2,0,1:T(8,128)(2,1)} %bitcast.9, bf16[3,1,160,384]{3,2,0,1:T(8,128)(2,1)S(1)} %bitcast.57, bf16[1,4,160,384]{3,2,0,1:T(8,128)(2,1)S(1)} %fusion.38, bf16[1,4,160,384]{3,2,0,1:T(8,128)(2,1)S(1)} %get-tuple-element.10, bf16[1,4,160,384]{3,2,0,1:T(8,128)(2,1)S(1)} %get-tuple-element.9), kind=kLoop, calls=%fused_computation.18 | loop fusion | flops 20155392 | bytes 4451328 | tf_op jit(solution)/shard_map/broadcast_in_dim | solution.py:100
  119.0 1.7 %pad.5 = bf16[3,6,1,168,384]{4,3,0,1,2:T(8,128)(2,1)} pad(bf16[3,6,1,162,384]{4,3,0,1,2:T(8,128)(2,1)S(1)} %fusion.11, bf16[]{:T(256)} %constant.43.clone.1), padding=0_0x0_0x0_0x0_6x0_0 | pad | bytes 4561922 | tf_op jit(solution)/shard_map/broadcast_in_dim | solution.py:100
  120.6 3.5 %reshape.137 = bf16[3,6,1,8,21,384]{5,4,3,0,1,2:T(8,128)(2,1)S(1)} reshape(bf16[3,6,1,168,384]{4,3,0,1,2:T(8,128)(2,1)} %pad.5) | data formatting | bytes 4644864 | tf_op jit(solution)/shard_map/conv_general_dilated | solution.py:99
  124.6 1.7 %copy-done.5 = bf16[3,3,3,384,192]{3,4,2,1,0:T(8,128)(2,1)S(1)} copy-done((bf16[3,3,3,384,192]{3,4,2,1,0:T(8,128)(2,1)S(1)}, bf16[3,3,3,384,192]{3,4,2,1,0:T(8,128)(2,1)}, u32[]{:S(2)}) %copy-start.5) | copy-done | bytes 3981336
  126.3 3.9 %fusion.21 = f32[1,4,8,21,192]{4,2,3,1,0:T(8,128)S(1)} fusion(bf16[3,3,3,384,192]{3,4,2,1,0:T(8,128)(2,1)S(1)} %copy-done.5, bf16[3,6,1,7,2,384]{5,3,4,1,0,2:T(8,128)(2,1)S(1)} %slice.19, bf16[3,6,1,8,21,384]{5,3,4,1,0,2:T(8,128)(2,1)S(1)} %copy.47, pred[8,21]{0,1:T(8,128)(4,1)S(1)} %copy-done.6), kind=kOutput, calls=%fused_computation.29 | convolution fusion | flops 2683201536 | bytes 7013544 | tf_op jit(solution)/shard_map/conv_general_dilated | solution.py:99
  (44 shorter events, 7.7 us)
Async XLA Ops:
  0.0 70.3 %copy-start = (bf16[384,384]{1,0:T(8,128)(2,1)S(1)}, bf16[384,384]{1,0:T(8,128)(2,1)}, u32[]{:S(2)}) copy-start(bf16[384,384]{1,0:T(8,128)(2,1)} %param.14) | copy-start | bytes 884740
  0.0 6.4 %copy-start.3 = (bf16[384]{0:T(512)(128)(2,1)S(1)}, bf16[384]{0:T(512)(128)(2,1)}, u32[]{:S(2)}) copy-start(bf16[384]{0:T(512)(128)(2,1)} %param.11) | copy-start | bytes 2308
  6.5 1.6 %collective-permute-start = (bf16[1,320,384]{2,1,0:T(8,128)(2,1)S(1)}, bf16[1,320,384]{2,1,0:T(8,128)(2,1)S(1)}, u32[]{:S(2)}, u32[]{:S(2)}) collective-permute-start(bf16[1,320,384]{2,1,0:T(8,128)(2,1)S(1)} %multiply_convert_fusion), channel_id=1, source_target_pairs={{0,1},{1,0},{4,5},{5,4},{8,9},{9,8},{12,13},{13,12},{2,3},{3,2},{6... | collective-permute-start | bytes 737288 | tf_op jit(solution)/shard_map/ppermute | solution.py:24
  8.3 14.6 %collective-permute-start.1 = (bf16[2,320,384]{2,1,0:T(8,128)(2,1)S(1)}, bf16[2,320,384]{2,1,0:T(8,128)(2,1)S(1)}, u32[]{:S(2)}, u32[]{:S(2)}) collective-permute-start(bf16[2,320,384]{2,1,0:T(8,128)(2,1)S(1)} %pad_maximum_fusion.2), channel_id=1, source_target_pairs={{0,4},{1,5},{4,0},{5,1},{8,12},{9,13},{12,8},{13,9},{2,6},{3,7},{6... | collective-permute-start | bytes 1474568 | tf_op jit(solution)/shard_map/ppermute | solution.py:24
  11.4 15.1 %copy-start.4 = (bf16[384]{0:T(512)(128)(2,1)S(1)}, bf16[384]{0:T(512)(128)(2,1)}, u32[]{:S(2)}) copy-start(bf16[384]{0:T(512)(128)(2,1)} %param.12) | copy-start | bytes 2308
  23.2 45.4 %collective-permute-start.2 = (bf16[4,320,384]{2,1,0:T(8,128)(2,1)S(1)}, bf16[4,320,384]{2,1,0:T(8,128)(2,1)}, u32[]{:S(2)}, u32[]{:S(2)}) collective-permute-start(bf16[4,320,384]{2,1,0:T(8,128)(2,1)S(1)} %pad_maximum_fusion.1), channel_id=1, source_target_pairs={{0,8},{1,9},{4,12},{5,13},{8,0},{9,1},{12,4},{13,5},{2,10},{3,11},... | collective-permute-start | bytes 2949128 | tf_op jit(solution)/shard_map/ppermute | solution.py:24
  76.8 4.2 %copy-start.2 = (bf16[384,384]{1,0:T(8,128)(2,1)S(1)}, bf16[384,384]{1,0:T(8,128)(2,1)}, u32[]{:S(2)}) copy-start(bf16[384,384]{1,0:T(8,128)(2,1)} %param.16) | copy-start | bytes 884740
  81.0 18.6 %copy-start.1 = (bf16[2,4,160,384]{3,2,1,0:T(8,128)(2,1)S(1)}, bf16[2,4,160,384]{3,2,1,0:T(8,128)(2,1)}, u32[]{:S(2)}) copy-start(bf16[2,4,160,384]{3,2,1,0:T(8,128)(2,1)} %param.10) | copy-start | bytes 2949124
  84.1 5.5 %collective-permute-start.3 = (bf16[1,4,160,384]{3,2,0,1:T(8,128)(2,1)S(1)}, bf16[1,4,160,384]{3,2,0,1:T(8,128)(2,1)}, u32[]{:S(2)}, u32[]{:S(2)}) collective-permute-start(bf16[1,4,160,384]{3,2,0,1:T(8,128)(2,1)S(1)} %fusion.38), channel_id=1, source_target_pairs={} | collective-permute-start | bytes 1474568 | tf_op jit(solution)/shard_map/ppermute | solution.py:39
  85.6 14.0 %collective-permute-start.4 = (bf16[1,4,160,384]{3,2,0,1:T(8,128)(2,1)S(1)}, bf16[1,4,160,384]{3,2,0,1:T(8,128)(2,1)}, u32[]{:S(2)}, u32[]{:S(2)}) collective-permute-start(bf16[1,4,160,384]{3,2,0,1:T(8,128)(2,1)S(1)} %fusion.38), channel_id=1, source_target_pairs={{0,2},{1,3},{4,6},{5,7},{8,10},{9,11},{12,14},{13,15},{16,18},{17,... | collective-permute-start | bytes 1474568 | tf_op jit(solution)/shard_map/ppermute | solution.py:39
  101.7 10.1 %collective-permute-start.5 = (bf16[3,1,160,384]{3,2,1,0:T(8,128)(2,1)}, bf16[3,1,160,384]{3,2,1,0:T(8,128)(2,1)S(1)}, u32[]{:S(2)}, u32[]{:S(2)}) collective-permute-start(bf16[3,1,160,384]{3,2,1,0:T(8,128)(2,1)} %get-tuple-element.7), channel_id=1, source_target_pairs={{0,4},{4,8},{8,12},{1,5},{5,9},{9,13},{2,6},{6,10},{10,14},{3,7},{... | collective-permute-start | bytes 1105928 | tf_op jit(solution)/shard_map/ppermute | solution.py:50
  104.2 11.7 %collective-permute-start.6 = (bf16[3,1,160,384]{3,2,1,0:T(8,128)(2,1)}, bf16[3,1,160,384]{3,2,1,0:T(8,128)(2,1)}, u32[]{:S(2)}, u32[]{:S(2)}) collective-permute-start(bf16[3,1,160,384]{3,2,1,0:T(8,128)(2,1)} %get-tuple-element.8), channel_id=1, source_target_pairs={{4,0},{8,4},{12,8},{5,1},{9,5},{13,9},{6,2},{10,6},{14,10},{7,3},{... | collective-permute-start | bytes 1105928 | tf_op jit(solution)/shard_map/ppermute | solution.py:52
  124.2 2.1 %copy-start.5 = (bf16[3,3,3,384,192]{3,4,2,1,0:T(8,128)(2,1)S(1)}, bf16[3,3,3,384,192]{3,4,2,1,0:T(8,128)(2,1)}, u32[]{:S(2)}) copy-start(bf16[3,3,3,384,192]{3,4,2,1,0:T(8,128)(2,1)} %param.17) | copy-start | bytes 11943940
  124.2 2.1 %copy-start.6 = (pred[8,21]{0,1:T(8,128)(4,1)S(1)}, pred[8,21]{0,1:T(8,128)(4,1)}, u32[]{:S(2)}) copy-start(pred[8,21]{0,1:T(8,128)(4,1)} %constant.51) | copy-start | bytes 508
